TPU v7x, 32 devices: a whole 2x2x4 slice. The times are simulated.
32 devices in a mesh: view: 8 (over z, x), head: 4 (over y, core).
Axes of the slice: x: 2, y: 2, z: 4, core: 2. Of those that a mesh axis runs over, the one named last changes fastest.
Arguments:
- features: bfloat16 [16384, 1024], P(('view', 'head')), may hold values from -6 to 6
- attend_weight: bfloat16 [2, 3, 1024, 1024], P(None, None, 'view', 'head'), may hold values from -0.1875 to 0.1875
- output_weight: bfloat16 [2, 1024, 1024], P(None, 'view'), may hold values from -0.1875 to 0.1875
- fast_init: bfloat16 [2, 16, 3, 64, 512], P(None, 'head', None, None, 'view'), may hold values from -0.75 to 0.75
- update_mask: int32 [8, 2048], P('view'), may hold values 0 or 1
Outputs:
- refined: bfloat16 [16384, 1024], P(('view', 'head'))
All inputs are finite; a program needn't handle non-finite values. No bound on the sum of `update_mask` on one device may be relied on, other than what follows from the above.
Results may differ from a plain program's by a relative error of at most 0.035.
Values may be sent and summed in bfloat16 or wider, within the bound.
No kernel may reach another device: no remote copies, remote signals or barrier semaphores. Data moves between devices by JAX's collectives and lax.ppermute only.
A program may use at most 64 MiB of HBM per device.

v0:
```python
import jax
import jax.numpy as jnp
from jax import lax
from jax.sharding import PartitionSpec as P

BLOCKS = 2
NS_STEPS = 5
newton_coeffs = (3.4445, -4.775, 2.0315)
learn_rate = 1.0
score_scale = 0.25


def normalize(values, epsilon):
    return values * lax.rsqrt(jnp.mean(values * values, axis=-1, keepdims=True) + epsilon)


def newton_step(current, gram_matrix):
    squared = jnp.einsum(
        "...de,...ef->...df", gram_matrix, gram_matrix, precision=lax.Precision.HIGHEST
    )
    polynomial = newton_coeffs[1] * gram_matrix + newton_coeffs[2] * squared
    return newton_coeffs[0] * current + jnp.einsum(
        "...de,...ef->...df", polynomial, current, precision=lax.Precision.HIGHEST
    )


def self_gram(current):
    return jnp.einsum("...df,...ef->...de", current, current, precision=lax.Precision.HIGHEST)


def fast_gradient(keys, values, mask, weights):
    first = jnp.einsum("thd,hdf->thf", keys, weights[:, 0], preferred_element_type=jnp.float32)
    third = jnp.einsum("thd,hdf->thf", keys, weights[:, 1], preferred_element_type=jnp.float32)
    sigma = jax.nn.sigmoid(first)
    hidden = (first * sigma * third).astype(jnp.bfloat16)
    target = (-(mask[:, None, None].astype(jnp.float32) * values.astype(jnp.float32))).astype(
        jnp.bfloat16
    )
    back = jnp.einsum("thd,hdf->thf", target, weights[:, 2], preferred_element_type=jnp.float32)
    d_third = (back * first * sigma).astype(jnp.bfloat16)
    d_first = (back * third * sigma * (1.0 + first * (1.0 - sigma))).astype(jnp.bfloat16)
    grad_first = jnp.einsum("thd,thf->hdf", keys, d_first, preferred_element_type=jnp.float32)
    grad_third = jnp.einsum("thd,thf->hdf", keys, d_third, preferred_element_type=jnp.float32)
    grad_last = jnp.einsum("thd,thf->hdf", target, hidden, preferred_element_type=jnp.float32)
    return jnp.stack([grad_first, grad_third, grad_last], axis=1)


def fast_apply(queries, weights):
    first = jnp.einsum("thd,hdf->thf", queries, weights[:, 0], preferred_element_type=jnp.float32)
    third = jnp.einsum("thd,hdf->thf", queries, weights[:, 1], preferred_element_type=jnp.float32)
    hidden = (first * jax.nn.sigmoid(first) * third).astype(jnp.bfloat16)
    output = jnp.einsum("thf,hdf->thd", hidden, weights[:, 2], preferred_element_type=jnp.float32)
    return normalize(output, 1e-05)


def shards(features, attend_weight, output_weight, fast_init, update_mask):
    stream = features
    view_dev, view_len = update_mask.shape
    heads_here = fast_init.shape[1]
    head_dim = fast_init.shape[3]
    rows_all = view_dev * view_len
    block = min(512, view_len)
    count = rows_all // block
    mask_blocks = update_mask.reshape(count, block)
    for layer in range(BLOCKS):
        normed = normalize(stream.astype(jnp.float32), 1e-05).astype(jnp.bfloat16)
        whole = lax.all_gather(normed, "head", axis=0, tiled=True)
        packed = jnp.einsum(
            "td,jdc->tjc",
            whole,
            lax.all_gather(attend_weight[layer], "view", axis=1, tiled=True),
            preferred_element_type=jnp.float32,
        ).astype(jnp.bfloat16)
        packed = packed.reshape(rows_all, 3, heads_here, head_dim)
        queries = normalize(packed[:, 0].astype(jnp.float32), 1e-05).astype(jnp.bfloat16)
        keys = normalize(packed[:, 1].astype(jnp.float32), 1e-05).astype(jnp.bfloat16)
        values = packed[:, 2]
        key_views = keys.reshape(view_dev, view_len, heads_here, head_dim)
        value_views = values.reshape(view_dev, view_len, heads_here, head_dim)
        query_blocks = jnp.moveaxis(
            queries.reshape(view_dev, view_len // block, block, heads_here, head_dim), 1, 0
        )

        def attend_block(query_block):
            scores = (
                jnp.einsum(
                    "vqhd,vkhd->vhqk", query_block, key_views, preferred_element_type=jnp.float32
                )
                * score_scale
            )
            expo = jnp.exp(scores)
            probs = (expo / jnp.sum(expo, axis=-1, keepdims=True)).astype(jnp.bfloat16)
            return jnp.einsum(
                "vhqk,vkhd->vqhd", probs, value_views, preferred_element_type=jnp.float32
            )

        attended = jnp.moveaxis(lax.map(attend_block, query_blocks), 0, 1).reshape(
            rows_all, heads_here, head_dim
        )
        local_fast = fast_init[layer]
        full_fast = lax.all_gather(local_fast, "view", axis=3, tiled=True)

        def accumulate(total, inputs):
            return (total + fast_gradient(inputs[0], inputs[1], inputs[2], full_fast), None)

        key_blocks = keys.reshape(count, block, heads_here, head_dim)
        value_blocks = values.reshape(count, block, heads_here, head_dim)
        gradients, _ = lax.scan(
            accumulate,
            jnp.zeros(full_fast.shape, jnp.float32),
            (key_blocks, value_blocks, mask_blocks),
        )
        summed = lax.psum(gradients.astype(jnp.bfloat16), "view").astype(jnp.float32)
        squares = jnp.sum(summed * summed, axis=(2, 3), keepdims=True)
        current = summed * lax.rsqrt(squares + 1e-06)
        for _ in range(NS_STEPS):
            current = newton_step(current, self_gram(current))
        updated = (full_fast.astype(jnp.float32) - learn_rate * current).astype(jnp.bfloat16)

        def apply_block(query_block):
            return fast_apply(query_block, updated)

        applied = lax.map(apply_block, queries.reshape(count, block, heads_here, head_dim)).reshape(
            rows_all, heads_here, head_dim
        )
        mixed = (attended + applied).astype(jnp.bfloat16).reshape(rows_all, heads_here * head_dim)
        regrouped = lax.all_to_all(mixed, "head", split_axis=0, concat_axis=1, tiled=True)
        projected = jnp.dot(
            regrouped,
            lax.all_gather(output_weight[layer], "view", axis=0, tiled=True),
            preferred_element_type=jnp.float32,
        )
        stream = (stream.astype(jnp.float32) + projected).astype(jnp.bfloat16)
    return stream


def solution(mesh):
    return jax.shard_map(
        shards,
        mesh=mesh,
        in_specs=(
            P(("view", "head"), None),
            P(None, None, "view", "head"),
            P(None, "view", None),
            P(None, "head", None, None, "view"),
            P("view", None),
        ),
        out_specs=P(("view", "head"), None),
        check_vma=False,
    )
```

profile of v0, /device:TPU:0, one launch (start us, length us, event | category | flops | bytes accessed | tf_op | source)
XLA Modules:
  0.0 636.8 jit_solution(1773703120889669409)
XLA Ops:
  11.7 44.0 %all-gather.1 = bf16[1,4,3,64,512]{3,1,2,0,4:T(4,128)(2,1)} all-gather(bf16[1,4,3,64,64]{3,1,2,0,4:T(4,128)(2,1)S(1)} %copy.61), channel_id=3, replica_groups=mesh['view'=8,'head'=4] {'view'}, dimensions={4}, use_global_device_ids=true | all-gather | bytes 884736 | tf_op jit(solution)/shard_map/all_gather | solution.py:101
  59.5 6.3 all-gather.17.cloned.1.call-done
  65.8 35.9 %all-gather.13.cloned.1.call-done = bf16[2048,1024]{1,0:T(8,128)(2,1)} async-done(((bf16[512,1024]{1,0:T(8,128)(2,1)}), bf16[2048,1024]{1,0:T(8,128)(2,1)}) %all-gather.13.cloned.1.call-update) | async-done | bytes 4194320 | tf_op jit(solution)/shard_map/all_gather | solution.py:67
  101.7 6.1 fusion.188
  111.3 3.7 reshape.323
  122.1 60.1 %while.66 = (s32[]{:T(128)}, f32[4,3,64,512]{3,2,0,1:T(8,128)S(1)}, bf16[4,512,4,64]{1,3,2,0:T(8,128)(2,1)}, s32[4,512]{1,0:T(4,128)S(1)}, bf16[4,512,4,64]{1,3,...) while((s32[]{:T(128)}, f32[4,3,64,512]{3,2,0,1:T(8,128)S(1)}, ...), condition=%wide.region_7.8_spmd.clone, body=%wide.region_6.7_spmd.clone.sunk | while | flops 830996992 | bytes 50605152 | solution.py:108
  185.3 3.4 copy.40
  199.0 31.0 %while.62 = (s32[]{:T(128)}, f32[4,1,512,4,64]{2,4,3,1,0:T(8,128)S(1)}, bf16[4,1,512,4,64]{2,4,3,1,0:T(8,128)(2,1)}, bf16[1,2048,4,64]{1,3,2,0:T(8,128)(2,1)S(1)}, bf16[1,2048,4,64]{1,3,2,0:T(8,128)(2,1)}, /*index=5*/s32[]{:T(128)}) while((s32[]{:T(128)}, f32[4,1,512,4,64]{2,4,3,1,0:T(8,128)S(1)}, bf16[4,1,512,4,64]{2,4,3,1,0:T(8,128)(2,1)}, ...), condition=%wide.region_5.6_spmd, body=%wide.region_3.5_spmd.sunk | while | flops 1094711296 | bytes 40649316 | solution.py:97
  199.0 4.0 fusion.368
  203.1 3.7 fusion.369
  206.8 4.0 fusion.368
  210.9 3.7 fusion.369
  214.6 4.0 fusion.368
  218.6 3.7 fusion.369
  222.3 4.0 fusion.368
  226.4 3.7 fusion.369
  230.0 28.5 %all-reduce.3.cloned.1.call-done = bf16[4,3,64,512]{3,2,1,0:T(8,128)(2,1)} async-done(((bf16[4,3,64,512]{3,2,1,0:T(8,128)(2,1)}), bf16[4,3,64,512]{3,2,1,0:T(8,128)(2,1)}) %all-reduce.3.cloned.1.call-update) | async-done | bytes 786448 | tf_op jit(solution)/shard_map/psum | solution.py:113
  260.1 3.3 fusion.214
  283.2 35.3 %while.63 = (s32[]{:T(128)}, f32[4,512,4,64]{1,3,2,0:T(8,128)}, bf16[4,512,4,64]{1,3,2,0:T(8,128)(2,1)}, bf16[4,3,64,512]{3,2,0,1:T(8,128)(2,1)}, s32[]{:T(128)}) while((s32[]{:T(128)}, f32[4,512,4,64]{1,3,2,0:T(8,128)}, bf16[4,512,4,64]{1,3,2,0:T(8,128)(2,1)}, bf16[4,3,64,512]{3,2,0,1:T(8,128)(2,1)}, s32[]{:T(128)}) %tuple.131), condition=%wide.region_12.13_spmd, body=%wide.region_10.12_spmd.sunk | while | flops 409339904 | bytes 11306557 | solution.py:123
  283.2 3.8 fusion.374
  287.0 4.1 multiply_reduce_fusion.8
  292.0 3.8 fusion.374
  295.8 4.2 multiply_reduce_fusion.8
  300.8 3.8 fusion.374
  304.6 4.1 multiply_reduce_fusion.8
  309.7 3.8 fusion.374
  313.4 4.2 multiply_reduce_fusion.8
  321.4 3.7 all-to-all-start
  325.1 14.3 %all-to-all-done = bf16[4,512,256]{1,2,0:T(8,128)(2,1)S(1)} async-done(((bf16[4,512,256]{1,2,0:T(8,128)(2,1)}), bf16[4,512,256]{1,2,0:T(8,128)(2,1)S(1)}, u32[]{:S(2)}, u32[]{:S(2)}) %all-to-all-start) | async-done | bytes 1048608 | tf_op jit(solution)/shard_map/all_to_all | solution.py:127
  344.9 38.5 %all-gather.4 = bf16[1,4,3,64,512]{3,1,2,0,4:T(4,128)(2,1)} all-gather(bf16[1,4,3,64,64]{3,1,2,0,4:T(4,128)(2,1)S(1)} %copy.63), channel_id=6, replica_groups=mesh['view'=8,'head'=4] {'view'}, dimensions={4}, use_global_device_ids=true | all-gather | bytes 884736 | tf_op jit(solution)/shard_map/all_gather | solution.py:101
  386.2 5.2 all-gather.15.cloned.1.call-done
  391.5 6.1 fusion.191
  400.9 3.6 reshape.327
  411.8 62.9 %while.67 = (s32[]{:T(128)}, f32[4,3,64,512]{3,2,0,1:T(8,128)S(1)}, bf16[4,512,4,64]{1,3,2,0:T(8,128)(2,1)}, s32[4,512]{1,0:T(4,128)}, bf16[4,512,4,64]{1,3,2,0:...) while((s32[]{:T(128)}, f32[4,3,64,512]{3,2,0,1:T(8,128)S(1)}, ...), condition=%wide.region_20.21_spmd.clone, body=%wide.region_19.20_spmd.clone.sunk | while | flops 830996992 | bytes 50605152 | solution.py:108
  422.9 3.0 fusion.415
  438.6 3.0 fusion.415
  454.4 3.0 fusion.415
  470.1 3.0 fusion.415
  476.5 3.5 copy.51
  486.5 3.2 fusion.208
  491.3 34.0 %while.64 = (s32[]{:T(128)}, f32[4,1,512,4,64]{2,4,3,1,0:T(8,128)}, bf16[4,1,512,4,64]{2,4,3,1,0:T(8,128)(2,1)}, bf16[1,2048,4,64]{1,3,2,0:T(8,128)(2,1)S(1)}, bf16[1,2048,4,64]{1,3,2,0:T(8,128)(2,1)}, /*index=5*/s32[]{:T(128)}) while((s32[]{:T(128)}, f32[4,1,512,4,64]{2,4,3,1,0:T(8,128)}, bf16[4,1,512,4,64]{2,4,3,1,0:T(8,128)(2,1)}, ...), condition=%wide.region_18.19_spmd, body=%wide.region_16.18_spmd.sunk | while | flops 1094711296 | bytes 40649824 | solution.py:97
  491.3 4.1 fusion.376
  495.4 4.3 fusion.377
  499.7 4.0 fusion.376
  503.8 4.3 fusion.377
  508.1 4.0 fusion.376
  512.2 4.3 fusion.377
  516.5 4.0 fusion.376
  520.5 4.3 fusion.377
  526.9 24.3 %all-reduce.5.cloned.1.call-done = bf16[4,3,64,512]{3,2,1,0:T(8,128)(2,1)} async-done(((bf16[4,3,64,512]{3,2,1,0:T(8,128)(2,1)}), bf16[4,3,64,512]{3,2,1,0:T(8,128)(2,1)}) %all-reduce.5.cloned.1.call-update) | async-done | bytes 786448 | tf_op jit(solution)/shard_map/psum | solution.py:113
  552.6 3.2 fusion.211
  573.2 31.6 %while.65 = (s32[]{:T(128)}, f32[4,512,4,64]{1,3,2,0:T(8,128)S(1)}, bf16[4,512,4,64]{1,3,2,0:T(8,128)(2,1)}, bf16[4,3,64,512]{3,2,0,1:T(8,128)(2,1)S(1)}, s32[]{:T(128)}) while((s32[]{:T(128)}, f32[4,512,4,64]{1,3,2,0:T(8,128)S(1)}, bf16[4,512,4,64]{1,3,2,0:T(8,128)(2,1)}, bf16[4,3,64,512]{3,2,0,1:T(8,128)(2,1)S(1)}, s32[]{:T(128)}) %tuple.140), condition=%wide.region_25.26_spmd, body=%wide.region_23.25_spmd.sunk | while | flops 409339904 | bytes 11306049 | solution.py:123
  573.2 3.7 fusion.382
  576.9 4.1 multiply_reduce_fusion.9
  581.1 3.7 fusion.382
  584.8 4.1 multiply_reduce_fusion.9
  589.0 3.7 fusion.382
  592.7 4.1 multiply_reduce_fusion.9
  596.9 3.7 fusion.382
  600.6 4.1 multiply_reduce_fusion.9
  604.8 3.1 fusion.202
  607.9 3.6 all-to-all-start.1
  611.6 14.4 %all-to-all-done.1 = bf16[4,512,256]{1,2,0:T(8,128)(2,1)S(1)} async-done(((bf16[4,512,256]{1,2,0:T(8,128)(2,1)}), bf16[4,512,256]{1,2,0:T(8,128)(2,1)S(1)}, u32[]{:S(2)}, u32[]{:S(2)}) %all-to-all-start.1) | async-done | bytes 1048608 | tf_op jit(solution)/shard_map/all_to_all | solution.py:127
  625.9 3.8 fusion.199
  (244 shorter events, 220.0 us)
Async XLA Ops:
  6.5 2.7 copy-start.7
  6.5 59.3 %all-gather.17.cloned.1.call-start = ((), (), s32[]{:S(2)}) async-start(), calls=%async_computation.6 | async-start | bytes 1769472 | tf_op jit(solution)/shard_map/all_gather | solution.py:71
  9.2 1.7 copy-start.20
  9.2 92.5 %all-gather.13.cloned.1.call-start = ((), (), s32[]{:S(2)}) async-start(), calls=%async_computation.2 | async-start | bytes 5242880 | tf_op jit(solution)/shard_map/all_gather | solution.py:67
  10.8 247.8 %all-reduce.3.cloned.1.call-start = ((), (), s32[]{:S(2)}) async-start(), calls=%async_computation.3 | async-start | bytes 1572864 | tf_op jit(solution)/shard_map/psum | solution.py:113
  11.7 47.1 %copy-start.22 = (s32[1,2048]{1,0:T(1,128)S(1)}, s32[1,2048]{1,0:T(1,128)}, u32[]{:S(2)}) copy-start(s32[1,2048]{1,0:T(1,128)} %param.21) | copy-start | bytes 24580
  107.9 3.3 copy-start.2
  182.2 2.0 copy-start.21
  182.2 1.1 copy-start.19
  182.3 2.2 copy-start.18
  183.3 5.4 copy-start
  183.3 141.8 %all-gather.19.cloned.1.call-start = ((), (), s32[]{:S(2)}) async-start(), calls=%async_computation.7 | async-start | bytes 2359296 | tf_op jit(solution)/shard_map/all_gather | solution.py:130
  184.3 202.0 %all-gather.21.cloned.1.call-start = ((), (), s32[]{:S(2)}) async-start(), calls=%async_computation.8 | async-start | bytes 1769472 | tf_op jit(solution)/shard_map/all_gather | solution.py:71
  193.6 1.9 copy-start.6
  195.5 1.6 copy-start.5
  199.0 4.1 copy-start.13
  206.8 4.1 copy-start.13
  214.5 4.1 copy-start.13
  222.3 4.1 copy-start.13
  258.6 5.3 copy-start.11
  276.9 2.1 copy-start.9
  321.4 18.1 %copy-start.8 = (bf16[512,1024]{1,0:T(8,128)(2,1)S(1)}, bf16[512,1024]{1,0:T(8,128)(2,1)}, u32[]{:S(2)}) copy-start(bf16[512,1024]{1,0:T(8,128)(2,1)} %param.17) | copy-start | bytes 3145732
  321.4 18.1 %all-to-all-start = ((bf16[4,512,256]{1,2,0:T(8,128)(2,1)}), bf16[4,512,256]{1,2,0:T(8,128)(2,1)S(1)}, u32[]{:S(2)}, u32[]{:S(2)}) async-start(bf16[4,512,256]{1,2,0:T(8,128)(2,1)} %fusion.206), calls=%async_computation | async-start | bytes 2097152 | tf_op jit(solution)/shard_map/all_to_all | solution.py:127
  325.1 66.4 %all-gather.15.cloned.1.call-start = ((), (), s32[]{:S(2)}) async-start(), calls=%async_computation.4 | async-start | bytes 5242880 | tf_op jit(solution)/shard_map/all_gather | solution.py:67
  342.4 1.0 copy-start.15
  342.4 2.3 copy-start.17
  344.7 206.5 %all-reduce.5.cloned.1.call-start = ((), (), s32[]{:S(2)}) async-start(), calls=%async_computation.5 | async-start | bytes 1572864 | tf_op jit(solution)/shard_map/psum | solution.py:113
  397.6 3.3 copy-start.3
  475.8 135.8 %all-gather.23.cloned.1.call-start = ((), (), s32[]{:S(2)}) async-start(), calls=%async_computation.9 | async-start | bytes 2359296 | tf_op jit(solution)/shard_map/all_gather | solution.py:130
  476.5 5.1 copy-start.1
  491.3 34.0 %copy-start.4 = (f32[4,512,4,64]{1,0,3,2:T(4,128)S(1)}, f32[4,512,4,64]{1,0,3,2:T(4,128)}, u32[]{:S(2)}) copy-start(f32[4,512,4,64]{1,0,3,2:T(4,128)} %reshape.326) | copy-start | bytes 6291460
  491.3 4.1 copy-start.14
  499.7 4.0 copy-start.14
  508.1 4.0 copy-start.14
  516.5 4.0 copy-start.14
  551.1 5.2 copy-start.12
  569.1 2.1 copy-start.10
  607.9 18.1 %copy-start.16 = (bf16[512,1024]{1,0:T(8,128)(2,1)S(1)}, bf16[512,1024]{1,0:T(8,128)(2,1)}, u32[]{:S(2)}) copy-start(bf16[512,1024]{1,0:T(8,128)(2,1)} %copy-done.15) | copy-start | bytes 3145732
  607.9 18.1 %all-to-all-start.1 = ((bf16[4,512,256]{1,2,0:T(8,128)(2,1)}), bf16[4,512,256]{1,2,0:T(8,128)(2,1)S(1)}, u32[]{:S(2)}, u32[]{:S(2)}) async-start(bf16[4,512,256]{1,2,0:T(8,128)(2,1)} %fusion.202), calls=%async_computation.1 | async-start | bytes 2097152 | tf_op jit(solution)/shard_map/all_to_all | solution.py:127
Sparse Core Ops, SparseCore 0:
  9.4 56.3 all-gather.16
  67.4 34.3 all-gather.12
  183.4 75.1 all-reduce.2
  260.6 48.2 all-gather.18
  310.8 45.6 all-gather.20
  357.8 33.5 all-gather.14
  475.9 75.2 all-reduce.4
  553.2 48.2 all-gather.22
where the time goes:
time: 649 us; the launch traced here: 637 us
  matrix products  294 us (45%)
  waiting for transfers between devices  130 us (20%)
  blocking collectives  82.5 us (13%)
  local copies, waits for them, and re-layouts  56.3 us (9%)
  other arithmetic  50.9 us (8%)
  between operations  14.3 us (2%)
  starting transfers between devices  7.77 us (1%)
    all_gather x2, blocking collectives, shards(): full_fast = lax.all_gather(local_fast, 'view', axis=3, tiled=True)  82.5 us
    psum x2, waiting for transfers between devices, shards(): lax.psum(gradients.astype(jnp.bfloat16), 'view').astype(jnp.float32)  52.8 us
    all_gather x2, waiting for transfers between devices, shards(): whole = lax.all_gather(normed, 'head', axis=0, tiled=True)  41.2 us
    dot_general x8, matrix products, fast_apply(): jnp.einsum('thf,hdf->thd', hidden, weights[:, 2], preferred_element_type=...  33 us
    dot_general x8, matrix products, attend_block(): jnp.einsum('vqhd,vkhd->vhqk', query_block, key_views, preferred_element_t...  32.4 us
    dot_general x8, matrix products, attend_block(): jnp.einsum('vhqk,vkhd->vqhd', probs, value_views, preferred_element_type=...  31.9 us
    dot_general x8, matrix products, fast_apply(): jnp.einsum('thd,hdf->thf', queries, weights[:, 0], preferred_element_type...  29.9 us
    all_to_all x2, waiting for transfers between devices, shards(): lax.all_to_all(mixed, 'head', split_axis=0, concat_axis=1, tiled=True)  28.7 us
  transfers between devices with their start and end apart: 10, of which 7 were waited for; matrix products, arithmetic and copies ran while one was open for 36% of the time, Pallas kernels for 0%

commit v1 on v0

--- a/solution.py
+++ b/solution.py
@@ -98,7 +98,8 @@
             rows_all, heads_here, head_dim
         )
         local_fast = fast_init[layer]
-        full_fast = lax.all_gather(local_fast, "view", axis=3, tiled=True)
+        y = jax.lax.all_gather(local_fast, "view")
+        full_fast = jnp.concatenate(y, axis=3)
 
         def accumulate(total, inputs):
             return (total + fast_gradient(inputs[0], inputs[1], inputs[2], full_fast), None)

time: 649 us -> 630 us (0.971); the launches traced: 637 us -> 625 us
  matrix products: 294 us -> 277 us
  waiting for transfers between devices: 130 us -> 139 us
    dot_general x8, matrix products: 24.3 us -> 11.8 us  [fast_gradient(): jnp.einsum('thd,thf->hdf', target, hidden, preferred_element_type=jnp.flo...]
    all_gather x4 -> x0, local copies, waits for them, and re-layouts: 12.4 us -> none  [shards(): full_fast = lax.all_gather(local_fast, 'view', axis=3, tiled=True)]
    psum x2, waiting for transfers between devices: 52.8 us -> 64.1 us  [shards(): lax.psum(gradients.astype(jnp.bfloat16), 'view').astype(jnp.float32)]
    reshape x0 -> x4, local copies, waits for them, and re-layouts: none -> 10.9 us  [shards(): full_fast = jnp.concatenate(y, axis=3)]
    dot_general x8, matrix products: 13.7 us -> 6.11 us  [fast_gradient(): jnp.einsum('thd,hdf->thf', target, weights[:, 2], preferred_element_type=...]
where the time goes in v1:
time: 630 us; the launch traced here: 625 us
  matrix products  277 us (44%)
  waiting for transfers between devices  139 us (22%)
  blocking collectives  80 us (13%)
  local copies, waits for them, and re-layouts  55.9 us (9%)
  other arithmetic  49.6 us (8%)
  between operations  14.4 us (2%)
  starting transfers between devices  7.59 us (1%)
    all_gather x2, blocking collectives, shards(): y = jax.lax.all_gather(local_fast, 'view')  80 us
    psum x2, waiting for transfers between devices, shards(): lax.psum(gradients.astype(jnp.bfloat16), 'view').astype(jnp.float32)  64.1 us
    all_gather x2, waiting for transfers between devices, shards(): whole = lax.all_gather(normed, 'head', axis=0, tiled=True)  38.5 us
    dot_general x8, matrix products, fast_apply(): jnp.einsum('thf,hdf->thd', hidden, weights[:, 2], preferred_element_type=...  33 us
    dot_general x8, matrix products, attend_block(): jnp.einsum('vqhd,vkhd->vhqk', query_block, key_views, preferred_element_t...  32.3 us
    dot_general x8, matrix products, fast_apply(): jnp.einsum('thd,hdf->thf', queries, weights[:, 0], preferred_element_type...  30 us
    dot_general x8, matrix products, attend_block(): jnp.einsum('vhqk,vkhd->vqhd', probs, value_views, preferred_element_type=...  29.3 us
    all_to_all x2, waiting for transfers between devices, shards(): lax.all_to_all(mixed, 'head', split_axis=0, concat_axis=1, tiled=True)  28.7 us
  transfers between devices with their start and end apart: 10, of which 7 were waited for; matrix products, arithmetic and copies ran while one was open for 36% of the time, Pallas kernels for 0%

profile of v1, /device:TPU:0, one launch (start us, length us, event | category | flops | bytes accessed | tf_op | source)
XLA Modules:
  0.0 624.7 jit_solution(1465987934055149510)
XLA Ops:
  12.7 42.3 %all_gather.26 = bf16[8,4,3,64,64]{4,3,2,1,0:T(8,128)(2,1)S(1)} all-gather(bf16[1,4,3,64,64]{4,3,2,1,0:T(8,128)(2,1)S(1)} %get-tuple-element.358), channel_id=1, replica_groups=mesh['view'=8,'head'=4] {'view'}, dimensions={0}, use_global_device_ids=true | all-gather | bytes 884736 | tf_op jit(solution)/shard_map/all_gather | solution.py:101
  60.4 6.5 %all-gather.15.cloned.1.call-done = bf16[1,3,1024,256]{2,3,1,0:T(8,128)(2,1)} async-done(((bf16[1,3,128,256]{2,3,1,0:T(8,128)(2,1)}), bf16[1,3,1024,256]{2,3,1,0:T(8,128)(2,1)}) %all-gather.15.cloned.1.call-update) | async-done | bytes 1572880 | tf_op jit(solution)/shard_map/all_gather | solution.py:71
  66.9 35.3 %all-gather.11.cloned.1.call-done = bf16[2048,1024]{1,0:T(8,128)(2,1)} async-done(((bf16[512,1024]{1,0:T(8,128)(2,1)}), bf16[2048,1024]{1,0:T(8,128)(2,1)}) %all-gather.11.cloned.1.call-update) | async-done | bytes 4194320 | tf_op jit(solution)/shard_map/all_gather | solution.py:67
  102.2 6.1 fusion.188
  112.2 3.7 reshape.339
  123.1 53.5 %while.66 = (s32[]{:T(128)}, f32[4,3,64,512]{3,2,0,1:T(8,128)S(1)}, bf16[4,512,4,64]{1,3,2,0:T(8,128)(2,1)}, s32[4,512]{1,0:T(4,128)S(1)}, bf16[4,512,4,64]{1,3,...) while((s32[]{:T(128)}, f32[4,3,64,512]{3,2,0,1:T(8,128)S(1)}, ...), condition=%wide.region_7.8_spmd.clone, body=%wide.region_6.7_spmd.clone.sunk | while | flops 830996992 | bytes 54796444 | solution.py:109
  131.3 3.5 fusion.400
  144.6 3.5 fusion.400
  157.9 3.5 fusion.400
  171.1 3.5 fusion.400
  189.8 31.0 %while.62 = (s32[]{:T(128)}, f32[4,1,512,4,64]{2,4,3,1,0:T(8,128)S(1)}, bf16[4,1,512,4,64]{2,4,3,1,0:T(8,128)(2,1)}, bf16[1,2048,4,64]{1,3,2,0:T(8,128)(2,1)S(1)}, bf16[1,2048,4,64]{1,3,2,0:T(8,128)(2,1)}, /*index=5*/s32[]{:T(128)}) while((s32[]{:T(128)}, f32[4,1,512,4,64]{2,4,3,1,0:T(8,128)S(1)}, bf16[4,1,512,4,64]{2,4,3,1,0:T(8,128)(2,1)}, ...), condition=%wide.region_5.6_spmd, body=%wide.region_3.5_spmd.sunk | while | flops 1094711296 | bytes 40648816 | solution.py:97
  189.8 4.0 fusion.368
  193.8 3.7 fusion.369
  197.5 4.0 fusion.368
  201.6 3.7 fusion.369
  205.3 4.0 fusion.368
  209.3 3.7 fusion.369
  213.0 4.0 fusion.368
  217.1 3.7 fusion.369
  220.8 32.2 %all-reduce.3.cloned.1.call-done = bf16[4,3,64,512]{3,2,1,0:T(8,128)(2,1)} async-done(((bf16[4,3,64,512]{3,2,1,0:T(8,128)(2,1)}), bf16[4,3,64,512]{3,2,1,0:T(8,128)(2,1)}) %all-reduce.3.cloned.1.call-update) | async-done | bytes 786448 | tf_op jit(solution)/shard_map/psum | solution.py:114
  277.4 35.6 %while.63 = (s32[]{:T(128)}, f32[4,512,4,64]{1,3,2,0:T(8,128)}, bf16[4,512,4,64]{1,3,2,0:T(8,128)(2,1)}, bf16[4,3,64,512]{3,2,0,1:T(8,128)(2,1)}, s32[]{:T(128)}) while((s32[]{:T(128)}, f32[4,512,4,64]{1,3,2,0:T(8,128)}, bf16[4,512,4,64]{1,3,2,0:T(8,128)(2,1)}, bf16[4,3,64,512]{3,2,0,1:T(8,128)(2,1)}, s32[]{:T(128)}) %tuple.131), condition=%wide.region_12.13_spmd, body=%wide.region_10.12_spmd.sunk | while | flops 409339904 | bytes 11305041 | solution.py:124
  277.4 3.8 fusion.374
  281.2 4.2 multiply_reduce_fusion.8
  286.3 3.8 fusion.374
  290.1 4.2 multiply_reduce_fusion.8
  295.1 3.8 fusion.374
  299.0 4.2 multiply_reduce_fusion.8
  304.1 3.8 fusion.374
  307.9 4.2 multiply_reduce_fusion.8
  315.9 3.7 all-to-all-start
  319.6 14.3 %all-to-all-done = bf16[4,512,256]{1,2,0:T(8,128)(2,1)S(1)} async-done(((bf16[4,512,256]{1,2,0:T(8,128)(2,1)}), bf16[4,512,256]{1,2,0:T(8,128)(2,1)S(1)}, u32[]{:S(2)}, u32[]{:S(2)}) %all-to-all-start) | async-done | bytes 1048608 | tf_op jit(solution)/shard_map/all_to_all | solution.py:128
  339.3 37.7 %all_gather.30 = bf16[8,4,3,64,64]{4,3,2,1,0:T(8,128)(2,1)S(1)} all-gather(bf16[1,4,3,64,64]{4,3,2,1,0:T(8,128)(2,1)S(1)} %copy-done.23), channel_id=1, replica_groups=mesh['view'=8,'head'=4] {'view'}, dimensions={0}, use_global_device_ids=true | all-gather | bytes 884736 | tf_op jit(solution)/shard_map/all_gather | solution.py:101
  382.7 3.2 all-gather.13.cloned.1.call-done
  385.9 6.1 fusion.191
  395.8 3.6 reshape.343
  406.6 56.0 %while.67 = (s32[]{:T(128)}, f32[4,3,64,512]{3,2,0,1:T(8,128)S(1)}, bf16[4,512,4,64]{1,3,2,0:T(8,128)(2,1)}, s32[4,512]{1,0:T(4,128)}, bf16[4,512,4,64]{1,3,2,0:...) while((s32[]{:T(128)}, f32[4,3,64,512]{3,2,0,1:T(8,128)S(1)}, ...), condition=%wide.region_20.21_spmd.clone, body=%wide.region_19.20_spmd.clone.sunk | while | flops 830996992 | bytes 54796444 | solution.py:109
  415.5 3.5 fusion.418
  429.5 3.5 fusion.418
  443.4 3.5 fusion.418
  457.4 3.5 fusion.418
  464.4 3.9 reshape.342
  476.1 31.0 %while.64 = (s32[]{:T(128)}, f32[4,1,512,4,64]{2,4,3,1,0:T(8,128)S(1)}, bf16[4,1,512,4,64]{2,4,3,1,0:T(8,128)(2,1)}, bf16[1,2048,4,64]{1,3,2,0:T(8,128)(2,1)S(1)}, bf16[1,2048,4,64]{1,3,2,0:T(8,128)(2,1)}, /*index=5*/s32[]{:T(128)}) while((s32[]{:T(128)}, f32[4,1,512,4,64]{2,4,3,1,0:T(8,128)S(1)}, bf16[4,1,512,4,64]{2,4,3,1,0:T(8,128)(2,1)}, ...), condition=%wide.region_18.19_spmd, body=%wide.region_16.18_spmd.sunk | while | flops 1094711296 | bytes 40648816 | solution.py:97
  476.1 4.0 fusion.376
  480.2 3.7 fusion.377
  483.9 4.0 fusion.376
  488.0 3.7 fusion.377
  491.7 4.0 fusion.376
  495.7 3.7 fusion.377
  499.4 4.0 fusion.376
  503.5 3.7 fusion.377
  507.2 31.9 %all-reduce.5.cloned.1.call-done = bf16[4,3,64,512]{3,2,1,0:T(8,128)(2,1)} async-done(((bf16[4,3,64,512]{3,2,1,0:T(8,128)(2,1)}), bf16[4,3,64,512]{3,2,1,0:T(8,128)(2,1)}) %all-reduce.5.cloned.1.call-update) | async-done | bytes 786448 | tf_op jit(solution)/shard_map/psum | solution.py:114
  540.5 3.2 fusion.211
  561.2 31.5 %while.65 = (s32[]{:T(128)}, f32[4,512,4,64]{1,3,2,0:T(8,128)S(1)}, bf16[4,512,4,64]{1,3,2,0:T(8,128)(2,1)}, bf16[4,3,64,512]{3,2,0,1:T(8,128)(2,1)S(1)}, s32[]{:T(128)}) while((s32[]{:T(128)}, f32[4,512,4,64]{1,3,2,0:T(8,128)S(1)}, bf16[4,512,4,64]{1,3,2,0:T(8,128)(2,1)}, bf16[4,3,64,512]{3,2,0,1:T(8,128)(2,1)S(1)}, s32[]{:T(128)}) %tuple.140), condition=%wide.region_25.26_spmd, body=%wide.region_23.25_spmd.sunk | while | flops 409339904 | bytes 11305041 | solution.py:124
  561.2 3.7 fusion.382
  564.9 4.1 multiply_reduce_fusion.9
  569.1 3.7 fusion.382
  572.8 4.1 multiply_reduce_fusion.9
  576.9 3.7 fusion.382
  580.6 4.1 multiply_reduce_fusion.9
  584.9 3.7 fusion.382
  588.6 4.1 multiply_reduce_fusion.9
  595.8 3.6 all-to-all-start.1
  599.5 14.4 %all-to-all-done.1 = bf16[4,512,256]{1,2,0:T(8,128)(2,1)S(1)} async-done(((bf16[4,512,256]{1,2,0:T(8,128)(2,1)}), bf16[4,512,256]{1,2,0:T(8,128)(2,1)S(1)}, u32[]{:S(2)}, u32[]{:S(2)}) %all-to-all-start.1) | async-done | bytes 1048608 | tf_op jit(solution)/shard_map/all_to_all | solution.py:128
  613.8 3.8 fusion.199
  (268 shorter events, 200.7 us)
Async XLA Ops:
  6.5 2.7 copy-start.15
  6.5 60.4 %all-gather.15.cloned.1.call-start = ((), (), s32[]{:S(2)}) async-start(), calls=%async_computation.6 | async-start | bytes 1769472 | tf_op jit(solution)/shard_map/all_gather | solution.py:71
  9.2 2.2 copy-start.28
  9.2 2.8 copy-start.26
  9.2 93.0 %all-gather.11.cloned.1.call-start = ((), (), s32[]{:S(2)}) async-start(), calls=%async_computation.2 | async-start | bytes 5242880 | tf_op jit(solution)/shard_map/all_gather | solution.py:67
  10.8 242.2 %all-reduce.3.cloned.1.call-start = ((), (), s32[]{:S(2)}) async-start(), calls=%async_computation.3 | async-start | bytes 1572864 | tf_op jit(solution)/shard_map/psum | solution.py:114
  60.3 48.0 %copy-start.9 = (bf16[4,3,64,512]{3,2,1,0:T(8,128)(2,1)}, bf16[4,3,64,512]{3,2,1,0:T(8,128)(2,1)S(1)}, u32[]{:S(2)}) copy-start(bf16[4,3,64,512]{3,2,1,0:T(8,128)(2,1)S(1)} %reshape.327) | copy-start | bytes 2359300
  108.4 3.3 copy-start.2
  124.8 1.8 copy-start.14
  138.1 1.8 copy-start.14
  151.4 1.8 copy-start.14
  164.6 1.8 copy-start.14
  176.6 2.0 copy-start.27
  176.6 1.1 copy-start.25
  176.6 2.0 copy-start.24
  177.7 1.8 copy-start
  177.7 141.9 %all-gather.17.cloned.1.call-start = ((), (), s32[]{:S(2)}) async-start(), calls=%async_computation.7 | async-start | bytes 2359296 | tf_op jit(solution)/shard_map/all_gather | solution.py:131
  178.6 204.1 %all-gather.19.cloned.1.call-start = ((), (), s32[]{:S(2)}) async-start(), calls=%async_computation.8 | async-start | bytes 1769472 | tf_op jit(solution)/shard_map/all_gather | solution.py:71
  184.3 1.9 copy-start.7
  186.2 1.6 copy-start.5
  189.8 4.1 copy-start.19
  197.5 4.1 copy-start.19
  205.3 4.1 copy-start.19
  213.0 4.1 copy-start.19
  253.0 5.2 copy-start.17
  271.1 2.1 copy-start.10
  315.9 18.1 %copy-start.16 = (bf16[512,1024]{1,0:T(8,128)(2,1)S(1)}, bf16[512,1024]{1,0:T(8,128)(2,1)}, u32[]{:S(2)}) copy-start(bf16[512,1024]{1,0:T(8,128)(2,1)} %param.17) | copy-start | bytes 3145732
  315.9 18.1 %all-to-all-start = ((bf16[4,512,256]{1,2,0:T(8,128)(2,1)}), bf16[4,512,256]{1,2,0:T(8,128)(2,1)S(1)}, u32[]{:S(2)}, u32[]{:S(2)}) async-start(bf16[4,512,256]{1,2,0:T(8,128)(2,1)} %fusion.206), calls=%async_computation | async-start | bytes 2097152 | tf_op jit(solution)/shard_map/all_to_all | solution.py:128
  319.5 66.3 %all-gather.13.cloned.1.call-start = ((), (), s32[]{:S(2)}) async-start(), calls=%async_computation.4 | async-start | bytes 5242880 | tf_op jit(solution)/shard_map/all_gather | solution.py:67
  336.9 1.0 copy-start.21
  336.9 2.4 copy-start.23
  339.2 199.8 %all-reduce.5.cloned.1.call-start = ((), (), s32[]{:S(2)}) async-start(), calls=%async_computation.5 | async-start | bytes 1572864 | tf_op jit(solution)/shard_map/psum | solution.py:114
  382.6 9.4 %copy-start.11 = (bf16[4,3,64,512]{3,2,1,0:T(8,128)(2,1)}, bf16[4,3,64,512]{3,2,1,0:T(8,128)(2,1)S(1)}, u32[]{:S(2)}) copy-start(bf16[4,3,64,512]{3,2,1,0:T(8,128)(2,1)S(1)} %reshape.332) | copy-start | bytes 2359300
  392.0 3.2 copy-start.3
  408.3 2.5 copy-start.13
  422.3 2.5 copy-start.13
  436.3 2.5 copy-start.13
  450.2 2.5 copy-start.13
  463.7 135.8 %all-gather.21.cloned.1.call-start = ((), (), s32[]{:S(2)}) async-start(), calls=%async_computation.9 | async-start | bytes 2359296 | tf_op jit(solution)/shard_map/all_gather | solution.py:131
  464.4 3.9 copy-start.1
  470.7 1.9 copy-start.6
  472.6 1.6 copy-start.4
  476.1 4.1 copy-start.20
  483.9 4.1 copy-start.20
  491.6 4.1 copy-start.20
  499.4 4.1 copy-start.20
  507.1 38.8 %copy-start.8 = (f32[4,1,512,4,64]{2,4,3,1,0:T(8,128)}, f32[4,1,512,4,64]{2,4,3,1,0:T(8,128)S(1)}, u32[]{:S(2)}) copy-start(f32[4,1,512,4,64]{2,4,3,1,0:T(8,128)S(1)} %get-tuple-element.170) | copy-start | bytes 6291460
  539.0 5.2 copy-start.18
  557.1 2.1 copy-start.12
  595.8 18.1 %copy-start.22 = (bf16[512,1024]{1,0:T(8,128)(2,1)S(1)}, bf16[512,1024]{1,0:T(8,128)(2,1)}, u32[]{:S(2)}) copy-start(bf16[512,1024]{1,0:T(8,128)(2,1)} %copy-done.21) | copy-start | bytes 3145732
  595.8 18.1 %all-to-all-start.1 = ((bf16[4,512,256]{1,2,0:T(8,128)(2,1)}), bf16[4,512,256]{1,2,0:T(8,128)(2,1)S(1)}, u32[]{:S(2)}, u32[]{:S(2)}) async-start(bf16[4,512,256]{1,2,0:T(8,128)(2,1)} %fusion.202), calls=%async_computation.1 | async-start | bytes 2097152 | tf_op jit(solution)/shard_map/all_to_all | solution.py:128
Sparse Core Ops, SparseCore 0:
  9.4 57.5 all-gather.14
  68.5 33.6 all-gather.10
  177.8 75.1 all-reduce.2
  255.0 48.2 all-gather.16
  305.1 45.6 all-gather.18
  352.2 33.5 all-gather.12
  463.8 75.2 all-reduce.4
  541.2 48.2 all-gather.20
